TPU v7x, 512 devices: a whole 4x8x8 slice. The times are simulated.
512 devices in a mesh: expert: 32 (over y, z_lo, core), tensor: 16 (over x, z_hi).
Axes of the slice: x: 4, y: 8, z: 8 (z_hi: 4, z_lo: 2; z = z_hi * 2 + z_lo), core: 2. Of those that a mesh axis runs over, the one named last changes fastest.
Arguments:
- tokens: bfloat16 [4096, 6144], P('expert', 'tensor'), may hold values from -6 to 6
- expert_ids: int32 [4096, 2], P('expert'), may hold values from 0 to 7, all different within a row; in each aligned block of 128 rows (0 to 127, 128 to 255, ...) at most 48 rows name the same one
- gate_fixed: int32 [4096, 2], P('expert'), may hold values from 4096 to 65535
- w_gate: bfloat16 [32, 1024, 6144], P('expert', None, 'tensor'), may hold values from -0.078125 to 0.078125
- w_up: bfloat16 [32, 1024, 6144], P('expert', None, 'tensor'), may hold values from -0.078125 to 0.078125
- w_down: bfloat16 [32, 1024, 6144], P('expert', None, 'tensor'), may hold values from -0.0625 to 0.0625
Outputs:
- mixed: bfloat16 [4096, 6144], P('expert', 'tensor')
Inputs may be any that keep to these rules, and one draw needn't show every extreme that they name: `expert_ids`: each row names 2 different experts. Among the 128 rows of one sequence shard (aligned blocks), no expert is named by more than 48 rows, a bound that some block reaches.
All inputs are finite; a program needn't handle non-finite values.
Results may differ from a plain program's by a relative error of at most 0.0064.
Values may be sent and summed in bfloat16 or wider, within the bound.
No kernel may reach another device: no remote copies, remote signals or barrier semaphores. Data moves between devices by JAX's collectives and lax.ppermute only.
A program may use at most 64 MiB of HBM per device.

v0:
```python
import jax
import jax.numpy as jnp
from jax import lax
from jax.sharding import PartitionSpec as P

EXPERTS = 4
CAP = 48


def on_device(tokens, expert_ids, gate_fixed, w_gate, w_up, w_down):
    width_part = tokens.shape[1]
    quarters = lax.axis_size("expert") // EXPERTS
    groups = lax.axis_size("tensor")
    expert_iota = jnp.arange(EXPERTS, dtype=jnp.int32)
    matched = expert_ids[:, :, None] == expert_iota
    routed = jnp.sum(matched.astype(jnp.int32), axis=1)
    weights = (
        jnp.sum(jnp.where(matched, gate_fixed[:, :, None], 0), axis=1).astype(jnp.float32) / 65536.0
    )
    position = jnp.cumsum(routed, axis=0) - routed
    slot_iota = jnp.arange(CAP, dtype=jnp.int32)
    placed = (position[:, :, None] == slot_iota) & (routed[:, :, None] > 0)
    outgoing = jnp.einsum(
        "tec,td->ecd", placed.astype(jnp.bfloat16), tokens, preferred_element_type=jnp.float32
    ).astype(jnp.bfloat16)
    outgoing = jnp.tile(outgoing, (quarters, 1, 1))
    arrived = lax.all_to_all(outgoing, "expert", split_axis=0, concat_axis=0, tiled=True)
    sources = arrived.shape[0]
    total_rows = sources * CAP
    rows_in = arrived.reshape(total_rows, width_part)
    gate_local = w_gate[0]
    up_local = w_up[0]
    down_local = w_down[0]
    hidden_width = gate_local.shape[0]
    contract = (((1,), (1,)), ((), ()))
    gate_term = lax.dot_general(
        rows_in, gate_local, contract, preferred_element_type=jnp.float32
    ).astype(jnp.bfloat16)
    up_term = lax.dot_general(
        rows_in, up_local, contract, preferred_element_type=jnp.float32
    ).astype(jnp.bfloat16)
    gate_parts, up_parts = (
        lax.all_to_all(gate_term, "tensor", split_axis=0, concat_axis=0, tiled=True),
        lax.all_to_all(up_term, "tensor", split_axis=0, concat_axis=0, tiled=True),
    )
    row_share = total_rows // groups
    gate_share = jnp.sum(
        gate_parts.reshape(groups, row_share, hidden_width).astype(jnp.float32), axis=0
    )
    up_share = jnp.sum(
        up_parts.reshape(groups, row_share, hidden_width).astype(jnp.float32), axis=0
    )
    hidden = (jax.nn.silu(gate_share) * up_share).astype(jnp.bfloat16)
    partial_out = jnp.dot(
        lax.all_gather(hidden, "tensor", axis=0, tiled=True),
        down_local,
        preferred_element_type=jnp.float32,
    )
    returned = lax.all_to_all(
        partial_out.reshape(sources, CAP, width_part),
        "expert",
        split_axis=0,
        concat_axis=0,
        tiled=True,
    )
    summed = jnp.sum(returned.reshape(quarters, EXPERTS, CAP, width_part), axis=0)
    selector = placed.astype(jnp.float32) * weights[:, :, None]
    mixed = jnp.einsum("tec,ecd->td", selector, summed, precision=lax.Precision.HIGHEST)
    return mixed.astype(jnp.bfloat16)


def solution(mesh):
    placed = (
        P("expert", "tensor"),
        P("expert", None),
        P("expert", None),
        P("expert", None, "tensor"),
        P("expert", None, "tensor"),
        P("expert", None, "tensor"),
    )
    return jax.shard_map(
        on_device, mesh=mesh, in_specs=placed, out_specs=P("expert", "tensor"), check_vma=False
    )
```

profile of v0, /device:TPU:1, one launch (start us, length us, event | category | flops | bytes accessed | tf_op | source)
XLA Modules:
  0.0 371.3 jit_solution(15921568439732790219)
XLA Ops:
  6.5 0.0 copy-start
  6.5 0.8 select_reduce_fusion
  7.3 0.1 copy.11
  7.4 0.2 reduce_window_sum.11
  7.6 0.1 copy.13
  7.7 1.1 convolution_convert_fusion.2
  8.8 0.1 tile.4
  8.9 41.6 %all_to_all.28 = bf16[32,48,384]{2,1,0:T(8,128)(2,1)S(1)} all-to-all(bf16[32,48,384]{2,1,0:T(8,128)(2,1)S(1)} %bitcast.28), channel_id=1, replica_groups=mesh['expert'=32,'tensor'=16] {'expert'}, dimensions={0} | all-to-all | bytes 2359296 | tf_op jit(solution)/shard_map/all_to_all | solution.py:27
  50.5 0.0 copy-done
  50.5 3.5 convolution_convert_fusion
  54.1 0.0 copy-start.1
  54.1 11.9 %all-to-all-start.2 = ((bf16[16,96,1024]{2,1,0:T(8,128)(2,1)}), bf16[16,96,1024]{2,1,0:T(8,128)(2,1)}, u32[]{:S(2)}, u32[]{:S(2)}) async-start(bf16[16,96,1024]{2,1,0:T(8,128)(2,1)} %bitcast.30), calls=%async_computation.2 | async-start | bytes 6291456 | tf_op jit(solution)/shard_map/all_to_all | solution.py:44
  66.0 0.0 copy-done.1
  66.0 3.5 convolution_convert_fusion.1
  69.5 58.6 %all-to-all-done.2 = bf16[16,96,1024]{2,1,0:T(8,128)(2,1)} async-done(((bf16[16,96,1024]{2,1,0:T(8,128)(2,1)}), bf16[16,96,1024]{2,1,0:T(8,128)(2,1)}, u32[]{:S(2)}, u32[]{:S(2)}) %all-to-all-start.2) | async-done | bytes 3145760 | tf_op jit(solution)/shard_map/all_to_all | solution.py:44
  128.1 16.4 %all-to-all-start.1 = ((bf16[16,96,1024]{2,1,0:T(8,128)(2,1)}), bf16[16,96,1024]{2,1,0:T(8,128)(2,1)}, u32[]{:S(2)}, u32[]{:S(2)}) async-start(bf16[16,96,1024]{2,1,0:T(8,128)(2,1)} %bitcast.29), calls=%async_computation.1 | async-start | bytes 6291456 | tf_op jit(solution)/shard_map/all_to_all | solution.py:43
  144.5 0.0 all-gather.2.cloned.1.call-start
  144.6 2.6 convert_reduce_fusion
  147.2 0.0 copy-start.2
  147.2 54.5 %all-to-all-done.1 = bf16[16,96,1024]{2,1,0:T(8,128)(2,1)} async-done(((bf16[16,96,1024]{2,1,0:T(8,128)(2,1)}), bf16[16,96,1024]{2,1,0:T(8,128)(2,1)}, u32[]{:S(2)}, u32[]{:S(2)}) %all-to-all-start.1) | async-done | bytes 3145760 | tf_op jit(solution)/shard_map/all_to_all | solution.py:43
  201.6 2.6 convert_reduce_fusion.1
  204.2 0.8 multiply_convert_fusion
  205.0 0.0 all-gather.2.cloned.1.call-update
  205.0 89.8 %all-gather.2.cloned.1.call-done = bf16[1536,1024]{1,0:T(8,128)(2,1)} async-done(((bf16[96,1024]{1,0:T(8,128)(2,1)}), bf16[1536,1024]{1,0:T(8,128)(2,1)}) %all-gather.2.cloned.1.call-update) | async-done | bytes 3145744 | tf_op jit(solution)/shard_map/all_gather | solution.py:55
  294.8 0.0 copy-done.2
  294.8 5.1 %fusion.1 = f32[32,48,384]{2,1,0:T(8,128)} fusion(bf16[32,48,1024]{2,1,0:T(8,128)(2,1)} %bitcast.33, bf16[1,1024,384]{2,1,0:T(8,128)(2,1)S(1)} %copy-done.2), kind=kOutput, calls=%fused_computation.7 | convolution fusion | flops 1207959552 | bytes 6291456 | tf_op jit(solution)/shard_map/dot_general | solution.py:54
  300.0 7.8 %all-to-all-start.3 = ((f32[32,48,384]{2,1,0:T(8,128)}), f32[32,48,384]{2,1,0:T(8,128)S(1)}, u32[]{:S(2)}, u32[]{:S(2)}) async-start(f32[32,48,384]{2,1,0:T(8,128)} %fusion.1), calls=%async_computation.3 | async-start | bytes 4718592 | tf_op jit(solution)/shard_map/all_to_all | solution.py:59
  307.8 55.5 %all-to-all-done.3 = f32[32,48,384]{2,1,0:T(8,128)S(1)} async-done(((f32[32,48,384]{2,1,0:T(8,128)}), f32[32,48,384]{2,1,0:T(8,128)S(1)}, u32[]{:S(2)}, u32[]{:S(2)}) %all-to-all-start.3) | async-done | bytes 2359328 | tf_op jit(solution)/shard_map/all_to_all | solution.py:59
  363.3 0.1 reduce_sum.49
  363.4 1.1 fusion
  (3 shorter events, 0.0 us)
Async XLA Ops:
  6.5 44.0 %copy-start = (bf16[1,1024,384]{2,1,0:T(8,128)(2,1)S(1)}, bf16[1,1024,384]{2,1,0:T(8,128)(2,1)}, u32[]{:S(2)}) copy-start(bf16[1,1024,384]{2,1,0:T(8,128)(2,1)} %param.10) | copy-start | bytes 2359300
  54.1 11.9 %copy-start.1 = (bf16[1,1024,384]{2,1,0:T(8,128)(2,1)S(1)}, bf16[1,1024,384]{2,1,0:T(8,128)(2,1)}, u32[]{:S(2)}) copy-start(bf16[1,1024,384]{2,1,0:T(8,128)(2,1)} %param.9) | copy-start | bytes 2359300
  54.1 74.1 %all-to-all-start.2 = ((bf16[16,96,1024]{2,1,0:T(8,128)(2,1)}), bf16[16,96,1024]{2,1,0:T(8,128)(2,1)}, u32[]{:S(2)}, u32[]{:S(2)}) async-start(bf16[16,96,1024]{2,1,0:T(8,128)(2,1)} %bitcast.30), calls=%async_computation.2 | async-start | bytes 6291456 | tf_op jit(solution)/shard_map/all_to_all | solution.py:44
  128.1 73.5 %all-to-all-start.1 = ((bf16[16,96,1024]{2,1,0:T(8,128)(2,1)}), bf16[16,96,1024]{2,1,0:T(8,128)(2,1)}, u32[]{:S(2)}, u32[]{:S(2)}) async-start(bf16[16,96,1024]{2,1,0:T(8,128)(2,1)} %bitcast.29), calls=%async_computation.1 | async-start | bytes 6291456 | tf_op jit(solution)/shard_map/all_to_all | solution.py:43
  144.5 150.3 %all-gather.2.cloned.1.call-start = ((), (), s32[]{:S(2)}) async-start(), calls=%async_computation.4 | async-start | bytes 3342336 | tf_op jit(solution)/shard_map/all_gather | solution.py:55
  147.2 147.7 %copy-start.2 = (bf16[1,1024,384]{2,1,0:T(8,128)(2,1)S(1)}, bf16[1,1024,384]{2,1,0:T(8,128)(2,1)}, u32[]{:S(2)}) copy-start(bf16[1,1024,384]{2,1,0:T(8,128)(2,1)} %param.11) | copy-start | bytes 2359300
  300.0 63.3 %all-to-all-start.3 = ((f32[32,48,384]{2,1,0:T(8,128)}), f32[32,48,384]{2,1,0:T(8,128)S(1)}, u32[]{:S(2)}, u32[]{:S(2)}) async-start(f32[32,48,384]{2,1,0:T(8,128)} %fusion.1), calls=%async_computation.3 | async-start | bytes 4718592 | tf_op jit(solution)/shard_map/all_to_all | solution.py:59
Sparse Core Ops, SparseCore 0:
  205.2 89.6 all-gather.1
where the time goes:
time: 372 us; the launch traced here: 371 us
  waiting for transfers between devices  258 us (69%)
  blocking collectives  41.6 us (11%)
  starting transfers between devices  36.1 us (10%)
  matrix products  14.4 us (4%)
  between operations  13.5 us (4%)
  other arithmetic  7.05 us (2%)
    all_gather x1, waiting for transfers between devices, on_device(): lax.all_gather(hidden, 'tensor', axis=0, tiled=True)  89.8 us
    all_to_all x1, waiting for transfers between devices, on_device(): lax.all_to_all(up_term, 'tensor', split_axis=0, concat_axis=0, tiled=True)  58.6 us
    all_to_all x1, waiting for transfers between devices, on_device(): lax.all_to_all(partial_out.reshape(sources, CAP, width_part), 'expert', s...  55.5 us
    all_to_all x1, waiting for transfers between devices, on_device(): lax.all_to_all(gate_term, 'tensor', split_axis=0, concat_axis=0, tiled=True)  54.5 us
    all_to_all x1, blocking collectives, on_device(): lax.all_to_all(outgoing, 'expert', split_axis=0, concat_axis=0, tiled=True)  41.6 us
    all_to_all x1, starting transfers between devices, on_device(): lax.all_to_all(gate_term, 'tensor', split_axis=0, concat_axis=0, tiled=True)  16.4 us
    all_to_all x1, starting transfers between devices, on_device(): lax.all_to_all(up_term, 'tensor', split_axis=0, concat_axis=0, tiled=True)  11.9 us
    all_to_all x1, starting transfers between devices, on_device(): lax.all_to_all(partial_out.reshape(sources, CAP, width_part), 'expert', s...  7.78 us
  transfers between devices with their start and end apart: 4, of which 4 were waited for; matrix products, arithmetic and copies ran while one was open for 2% of the time, Pallas kernels for 0%

commit v1 on v0

--- a/solution.py
+++ b/solution.py
@@ -52,7 +52,9 @@
     )
     hidden = (jax.nn.silu(gate_share) * up_share).astype(jnp.bfloat16)
     partial_out = jnp.dot(
-        lax.all_gather(hidden, "tensor", axis=0, tiled=True),
+        jnp.concatenate(
+            lax.all_to_all(jnp.stack([hidden] * lax.axis_size("tensor")), "tensor", 0, 0), axis=0
+        ),
         down_local,
         preferred_element_type=jnp.float32,
     )

time: 372 us -> 359 us (0.965)
  waiting for transfers between devices: 258 us -> 169 us
  blocking collectives: 41.6 us -> 121 us
  between operations: 13.5 us -> 0.1 us
  starting transfers between devices: 36.1 us -> 49.3 us
    all_gather x1 -> x0, waiting for transfers between devices: 89.8 us -> none  [on_device(): lax.all_gather(hidden, 'tensor', axis=0, tiled=True)]
    all_to_all x0 -> x1, blocking collectives: none -> 79.5 us  [on_device(): lax.all_to_all(jnp.stack([hidden] * lax.axis_size('tensor')), 'tensor', 0...]
    all_to_all x1, starting transfers between devices: 7.78 us -> 21 us  [on_device(): lax.all_to_all(partial_out.reshape(sources, CAP, width_part), 'expert', s...]
  transfers between devices with their start and end apart: 4 -> 3, of which waited for: 4 -> 3; matrix products, arithmetic and copies ran while one was open for 2% -> 2% of each run, Pallas kernels for 0% -> 0%
where the time goes in v1:
time: 359 us
  waiting for transfers between devices  169 us (47%)
  blocking collectives  121 us (34%)
  starting transfers between devices  49.3 us (14%)
  matrix products  12.5 us (3%)
  other arithmetic  6.36 us (2%)
    all_to_all x1, blocking collectives, on_device(): lax.all_to_all(jnp.stack([hidden] * lax.axis_size('tensor')), 'tensor', 0...  79.5 us
    all_to_all x1, waiting for transfers between devices, on_device(): lax.all_to_all(up_term, 'tensor', split_axis=0, concat_axis=0, tiled=True)  58.6 us
    all_to_all x1, waiting for transfers between devices, on_device(): lax.all_to_all(partial_out.reshape(sources, CAP, width_part), 'expert', s...  55.5 us
    all_to_all x1, waiting for transfers between devices, on_device(): lax.all_to_all(gate_term, 'tensor', split_axis=0, concat_axis=0, tiled=True)  54.5 us
    all_to_all x1, blocking collectives, on_device(): lax.all_to_all(outgoing, 'expert', split_axis=0, concat_axis=0, tiled=True)  41.6 us
    all_to_all x1, starting transfers between devices, on_device(): lax.all_to_all(partial_out.reshape(sources, CAP, width_part), 'expert', s...  21 us
    all_to_all x1, starting transfers between devices, on_device(): lax.all_to_all(gate_term, 'tensor', split_axis=0, concat_axis=0, tiled=True)  16.4 us
    all_to_all x1, starting transfers between devices, on_device(): lax.all_to_all(up_term, 'tensor', split_axis=0, concat_axis=0, tiled=True)  11.9 us
  transfers between devices with their start and end apart: 3, of which 3 were waited for; matrix products, arithmetic and copies ran while one was open for 2% of the time, Pallas kernels for 0%

profile of v1, /device:TPU:1, one launch (start us, length us, event | category | flops | bytes accessed | tf_op | source)
XLA Modules:
  0.0 358.6 jit_solution(17424086133381151937)
XLA Ops:
  0.0 0.0 copy-start
  0.0 0.8 select_reduce_fusion
  0.8 0.1 copy.11
  0.9 0.2 reduce_window_sum.11
  1.1 0.1 copy.13
  1.1 1.1 convolution_convert_fusion.2
  2.3 0.1 tile.4
  2.4 41.6 %all_to_all.33 = bf16[32,48,384]{2,1,0:T(8,128)(2,1)S(1)} all-to-all(bf16[32,48,384]{2,1,0:T(8,128)(2,1)S(1)} %bitcast.28), channel_id=1, replica_groups=mesh['expert'=32,'tensor'=16] {'expert'}, dimensions={0} | all-to-all | bytes 2359296 | tf_op jit(solution)/shard_map/all_to_all | solution.py:27
  44.0 0.0 copy-done
  44.0 3.5 convolution_convert_fusion
  47.5 0.0 copy-start.1
  47.5 11.9 %all-to-all-start.2 = ((bf16[16,96,1024]{2,1,0:T(8,128)(2,1)}), bf16[16,96,1024]{2,1,0:T(8,128)(2,1)}, u32[]{:S(2)}, u32[]{:S(2)}) async-start(bf16[16,96,1024]{2,1,0:T(8,128)(2,1)} %bitcast.30), calls=%async_computation.2 | async-start | bytes 6291456 | tf_op jit(solution)/shard_map/all_to_all | solution.py:44
  59.4 0.0 copy-done.1
  59.4 3.5 convolution_convert_fusion.1
  63.0 58.6 %all-to-all-done.2 = bf16[16,96,1024]{2,1,0:T(8,128)(2,1)} async-done(((bf16[16,96,1024]{2,1,0:T(8,128)(2,1)}), bf16[16,96,1024]{2,1,0:T(8,128)(2,1)}, u32[]{:S(2)}, u32[]{:S(2)}) %all-to-all-start.2) | async-done | bytes 3145760 | tf_op jit(solution)/shard_map/all_to_all | solution.py:44
  121.6 16.4 %all-to-all-start.1 = ((bf16[16,96,1024]{2,1,0:T(8,128)(2,1)}), bf16[16,96,1024]{2,1,0:T(8,128)(2,1)}, u32[]{:S(2)}, u32[]{:S(2)}) async-start(bf16[16,96,1024]{2,1,0:T(8,128)(2,1)} %bitcast.29), calls=%async_computation.1 | async-start | bytes 6291456 | tf_op jit(solution)/shard_map/all_to_all | solution.py:43
  138.0 2.6 convert_reduce_fusion
  140.6 54.5 %all-to-all-done.1 = bf16[16,96,1024]{2,1,0:T(8,128)(2,1)} async-done(((bf16[16,96,1024]{2,1,0:T(8,128)(2,1)}), bf16[16,96,1024]{2,1,0:T(8,128)(2,1)}, u32[]{:S(2)}, u32[]{:S(2)}) %all-to-all-start.1) | async-done | bytes 3145760 | tf_op jit(solution)/shard_map/all_to_all | solution.py:43
  195.1 2.6 convert_reduce_fusion.1
  197.7 0.1 multiply_convert_fusion
  197.8 0.4 stack.2
  198.2 0.0 copy-start.2
  198.2 79.5 %all_to_all.34 = bf16[16,96,1024]{2,1,0:T(8,128)(2,1)S(1)} all-to-all(bf16[16,96,1024]{2,1,0:T(8,128)(2,1)S(1)} %stack.2), channel_id=1, replica_groups=mesh['expert'=32,'tensor'=16] {'tensor'}, dimensions={0} | all-to-all | bytes 6291456 | tf_op jit(solution)/shard_map/all_to_all | solution.py:56
  277.7 0.0 copy-done.2
  277.7 3.2 fusion.1
  280.9 21.0 %all-to-all-start.4 = ((f32[32,48,384]{2,1,0:T(8,128)}), f32[32,48,384]{2,1,0:T(8,128)S(1)}, u32[]{:S(2)}, u32[]{:S(2)}) async-start(f32[32,48,384]{2,1,0:T(8,128)} %fusion.1), calls=%async_computation.4 | async-start | bytes 4718592 | tf_op jit(solution)/shard_map/all_to_all | solution.py:61
  301.9 55.5 %all-to-all-done.4 = f32[32,48,384]{2,1,0:T(8,128)S(1)} async-done(((f32[32,48,384]{2,1,0:T(8,128)}), f32[32,48,384]{2,1,0:T(8,128)S(1)}, u32[]{:S(2)}, u32[]{:S(2)}) %all-to-all-start.4) | async-done | bytes 2359328 | tf_op jit(solution)/shard_map/all_to_all | solution.py:61
  357.4 0.1 reduce_sum.49
  357.6 1.1 fusion
  (3 shorter events, 0.0 us)
Async XLA Ops:
  0.0 44.0 %copy-start = (bf16[1,1024,384]{2,1,0:T(8,128)(2,1)S(1)}, bf16[1,1024,384]{2,1,0:T(8,128)(2,1)}, u32[]{:S(2)}) copy-start(bf16[1,1024,384]{2,1,0:T(8,128)(2,1)} %param.10) | copy-start | bytes 2359300
  47.5 11.9 %copy-start.1 = (bf16[1,1024,384]{2,1,0:T(8,128)(2,1)S(1)}, bf16[1,1024,384]{2,1,0:T(8,128)(2,1)}, u32[]{:S(2)}) copy-start(bf16[1,1024,384]{2,1,0:T(8,128)(2,1)} %param.9) | copy-start | bytes 2359300
  47.5 74.1 %all-to-all-start.2 = ((bf16[16,96,1024]{2,1,0:T(8,128)(2,1)}), bf16[16,96,1024]{2,1,0:T(8,128)(2,1)}, u32[]{:S(2)}, u32[]{:S(2)}) async-start(bf16[16,96,1024]{2,1,0:T(8,128)(2,1)} %bitcast.30), calls=%async_computation.2 | async-start | bytes 6291456 | tf_op jit(solution)/shard_map/all_to_all | solution.py:44
  121.6 73.5 %all-to-all-start.1 = ((bf16[16,96,1024]{2,1,0:T(8,128)(2,1)}), bf16[16,96,1024]{2,1,0:T(8,128)(2,1)}, u32[]{:S(2)}, u32[]{:S(2)}) async-start(bf16[16,96,1024]{2,1,0:T(8,128)(2,1)} %bitcast.29), calls=%async_computation.1 | async-start | bytes 6291456 | tf_op jit(solution)/shard_map/all_to_all | solution.py:43
  198.2 79.5 %copy-start.2 = (bf16[1,1024,384]{2,1,0:T(8,128)(2,1)S(1)}, bf16[1,1024,384]{2,1,0:T(8,128)(2,1)}, u32[]{:S(2)}) copy-start(bf16[1,1024,384]{2,1,0:T(8,128)(2,1)} %param.11) | copy-start | bytes 2359300
  280.9 76.5 %all-to-all-start.4 = ((f32[32,48,384]{2,1,0:T(8,128)}), f32[32,48,384]{2,1,0:T(8,128)S(1)}, u32[]{:S(2)}, u32[]{:S(2)}) async-start(f32[32,48,384]{2,1,0:T(8,128)} %fusion.1), calls=%async_computation.4 | async-start | bytes 4718592 | tf_op jit(solution)/shard_map/all_to_all | solution.py:61
